TPU v7x, 32 devices: a whole 2x2x4 slice. The times are simulated.
32 devices in a mesh: groups: 2 (over y), node: 4 (over z), rep: 4 (over x, core).
Axes of the slice: x: 2, y: 2, z: 4, core: 2. Of those that a mesh axis runs over, the one named last changes fastest.
Arguments:
- node_states: bfloat16 [8, 512, 512], P(('groups', 'rep'), 'node'), parts along dimension 0, may hold values from -6 to 6
- cotangent: bfloat16 [8, 512, 512], P(('groups', 'rep'), 'node'), parts along dimension 0, may hold values from -1.1953125 to 1.1953125
- reach_blocks: int32 [8, 8, 8], P(('groups', 'rep'), 'node'), parts along dimension 0, may hold values from 0 to 7, as said below
- reach_count: int32 [8, 8], P(('groups', 'rep'), 'node'), parts along dimension 0, may hold values from 1 to 8, as said below
- level_start: int32 [8, 17], P(('groups', 'rep')), parts along dimension 0, may hold values from 0 to 512, as said below
- query_weight: bfloat16 [512, 256], replicated, may hold values from -0.25 to 0.25
- key_weight: bfloat16 [512, 256], replicated, may hold values from -0.25 to 0.25
- value_weight: bfloat16 [512, 256], replicated, may hold values from -0.25 to 0.25
- out_weight: bfloat16 [256, 512], replicated, may hold values from -0.375 to 0.375
- bias_table: float32 [4, 32], replicated, may hold values from -4 to 412
Outputs:
- updated: bfloat16 [8, 512, 512], P(('groups', 'rep'), 'node'), parts along dimension 0
- node_state_gradient: bfloat16 [8, 512, 512], P(('groups', 'rep'), 'node'), parts along dimension 0
- grad_query: float32 [1024, 256], P('groups'), parts along dimension 0
- grad_key: float32 [1024, 256], P('groups'), parts along dimension 0
- grad_value: float32 [1024, 256], P('groups'), parts along dimension 0
- grad_out: float32 [512, 512], P('groups'), parts along dimension 0
There are 2 independent parts, one for each index of `groups`. A program takes and returns all parts, laid end to end along the dimension named above; an argument that names none is the same for every part. Nothing has to cross between parts.
Inputs may be any that keep to these rules, and one draw needn't show every extreme that they name: `reach_blocks`: in row b of a graph, entry 0 is b, entries 1 to min(b, 7) are distinct blocks below b, and any later entries are b. `reach_count`: row b holds at most b + 1; row 7 of every graph holds 8. `level_start`: strictly increasing; entry 0 is 0 and entry 16 is 512.
All inputs are finite; a program needn't handle non-finite values.
Results may differ from a plain program's by a relative error of at most 0.011.
Values may be sent and summed in bfloat16 or wider, within the bound.
No kernel may reach another device: no remote copies, remote signals or barrier semaphores. Data moves between devices by JAX's collectives and lax.ppermute only.
A program may use at most 64 MiB of HBM per device.

v0:
```python
import jax
import jax.numpy as jnp
from jax import lax
from jax.sharding import PartitionSpec as P

HEADS = 4
HEAD = 64
BLOCK = 64
DIST = 32
EPS = 1e-05
NEG = -1e30
HIGH = lax.Precision.HIGHEST
CONTRACT_ROWS = (((0,), (0,)), ((), ()))
CONTRACT_COLS = (((1,), (1,)), ((), ()))


def rows_product(left, right):
    return lax.dot_general(left, right, CONTRACT_ROWS, preferred_element_type=jnp.float32)


def cols_product(left, right):
    return lax.dot_general(left, right, CONTRACT_COLS, preferred_element_type=jnp.float32)


def expand(listed):
    return jnp.repeat(jnp.repeat(listed, BLOCK, axis=0), BLOCK, axis=1)


def level_tables(starts, total, bias_table):
    level_count = starts.shape[0] - 1
    places = jnp.arange(total, dtype=jnp.int32)
    inner = starts[1:level_count]
    levels = jnp.sum((places[:, None] >= inner[None, :]).astype(jnp.int32), axis=1)
    marks = jnp.arange(level_count, dtype=jnp.int32)
    onehot = (levels[:, None] == marks[None, :]).astype(jnp.float32)
    spread = jnp.clip(marks[:, None] - marks[None, :], 0, DIST - 1)
    picks = (spread[:, :, None] == jnp.arange(DIST, dtype=jnp.int32)[None, None, :]).astype(
        jnp.float32
    )
    level_bias = jnp.einsum("hd,abd->hab", bias_table, picks, precision=HIGH)
    return (levels, onehot, level_bias)


def bias_block(row_onehot, head_bias, col_onehot):
    row_part = jnp.dot(row_onehot, head_bias, precision=HIGH)
    return lax.dot_general(row_part, col_onehot, CONTRACT_COLS, precision=HIGH)


def on_device(
    node_states,
    cotangent,
    reach_blocks,
    reach_count,
    level_start,
    query_weight,
    key_weight,
    value_weight,
    out_weight,
    bias_table,
):
    states = node_states[0]
    grads_in = cotangent[0]
    blocks = reach_blocks[0]
    counts = reach_count[0]
    starts = level_start[0]
    rows_dev = states.shape[0]
    width = query_weight.shape[1]
    total = rows_dev * lax.axis_size("node")
    offset = lax.axis_index("node") * rows_dev
    scale = HEAD ** (-0.5)
    key_blocks = total // BLOCK
    states_single_float = states.astype(jnp.float32)
    inverse_norm_scale = lax.rsqrt(
        jnp.mean(states_single_float * states_single_float, axis=1, keepdims=True) + EPS
    )
    centered_states = states_single_float * inverse_norm_scale
    normalized_states = centered_states.astype(jnp.bfloat16)
    queries = jnp.dot(normalized_states, query_weight, preferred_element_type=jnp.float32).astype(
        jnp.bfloat16
    )
    keys = jnp.dot(normalized_states, key_weight, preferred_element_type=jnp.float32).astype(
        jnp.bfloat16
    )
    values = jnp.dot(normalized_states, value_weight, preferred_element_type=jnp.float32).astype(
        jnp.bfloat16
    )
    keys_all, values_all = (
        lax.all_gather(keys, "node", axis=0, tiled=True),
        lax.all_gather(values, "node", axis=0, tiled=True),
    )
    levels, onehot, level_bias = level_tables(starts, total, bias_table)
    positions = jnp.arange(total, dtype=jnp.int32)
    local = jnp.arange(rows_dev, dtype=jnp.int32)
    row_ids = offset + local
    row_levels = lax.dynamic_slice_in_dim(levels, offset, rows_dev, 0)
    row_onehot = lax.dynamic_slice_in_dim(onehot, offset, rows_dev, 0)
    slots = jnp.arange(blocks.shape[1], dtype=jnp.int32)
    live = slots[None, :] < counts[:, None]
    kinds = jnp.arange(key_blocks, dtype=jnp.int32)
    listed = jnp.any((blocks[:, :, None] == kinds[None, None, :]) & live[:, :, None], axis=1)
    visible = expand(listed) & (
        (levels[None, :] < row_levels[:, None]) | (positions[None, :] == row_ids[:, None])
    )
    prob_list = []
    lse_list = []
    mixed_list = []
    for head in range(HEADS):
        lower = head * HEAD
        scores = (
            cols_product(queries[:, lower : lower + HEAD], keys_all[:, lower : lower + HEAD])
            * scale
        )
        scores = scores + bias_block(row_onehot, level_bias[head], onehot)
        scores = jnp.where(visible, scores, NEG)
        peak = jnp.max(scores, axis=1, keepdims=True)
        mass = jnp.sum(jnp.where(visible, jnp.exp(scores - peak), 0.0), axis=1, keepdims=True)
        lse = peak + jnp.log(mass)
        probs = jnp.where(visible, jnp.exp(scores - lse), 0.0).astype(jnp.bfloat16)
        prob_list.append(probs)
        lse_list.append(lse)
        mixed_list.append(
            jnp.dot(probs, values_all[:, lower : lower + HEAD], preferred_element_type=jnp.float32)
        )
    mixed = jnp.concatenate(mixed_list, axis=1).astype(jnp.bfloat16)
    updated = (
        states_single_float + jnp.dot(mixed, out_weight, preferred_element_type=jnp.float32)
    ).astype(jnp.bfloat16)
    partial_out = rows_product(mixed, grads_in)
    d_mixed = cols_product(grads_in, out_weight).astype(jnp.bfloat16)
    score_grads = []
    delta_list = []
    query_grads = []
    for head in range(HEADS):
        lower = head * HEAD
        mixed_head = d_mixed[:, lower : lower + HEAD]
        delta = jnp.sum(
            mixed_head.astype(jnp.float32) * mixed[:, lower : lower + HEAD].astype(jnp.float32),
            axis=1,
            keepdims=True,
        )
        d_probs = cols_product(mixed_head, values_all[:, lower : lower + HEAD])
        d_scores = (prob_list[head].astype(jnp.float32) * (d_probs - delta)).astype(jnp.bfloat16)
        score_grads.append(d_scores)
        delta_list.append(delta)
        query_grads.append(
            jnp.dot(d_scores, keys_all[:, lower : lower + HEAD], preferred_element_type=jnp.float32)
            * scale
        )
    d_queries = jnp.concatenate(query_grads, axis=1).astype(jnp.bfloat16)
    key_pieces = []
    value_pieces = []
    for head in range(HEADS):
        lower = head * HEAD
        score_part = score_grads[head]
        prob_part = prob_list[head]
        key_pieces.append(rows_product(score_part, queries[:, lower : lower + HEAD]) * scale)
        value_pieces.append(rows_product(prob_part, d_mixed[:, lower : lower + HEAD]))
    key_value_grads = lax.psum_scatter(
        jnp.concatenate(key_pieces + value_pieces, axis=1).astype(jnp.bfloat16),
        "node",
        scatter_dimension=0,
        tiled=True,
    ).astype(jnp.float32)
    d_keys = key_value_grads[:, :width].astype(jnp.bfloat16)
    d_values = key_value_grads[:, width:].astype(jnp.bfloat16)
    normalized_gradient = (
        cols_product(d_queries, query_weight)
        + cols_product(d_keys, key_weight)
        + cols_product(d_values, value_weight)
    )
    node_state_gradient = (
        grads_in.astype(jnp.float32)
        + inverse_norm_scale
        * (
            normalized_gradient
            - centered_states
            * jnp.mean(normalized_gradient * centered_states, axis=1, keepdims=True)
        )
    ).astype(jnp.bfloat16)
    partial_query = rows_product(normalized_states, d_queries)
    partial_key = rows_product(normalized_states, d_keys)
    partial_value = rows_product(normalized_states, d_values)
    total_query, total_key, total_value, total_out = lax.psum(
        (partial_query, partial_key, partial_value, partial_out), ("node", "rep")
    )
    return (
        updated[None],
        node_state_gradient[None],
        total_query,
        total_key,
        total_value,
        total_out,
    )


def solution(mesh):
    in_specs = (
        P(("groups", "rep"), "node", None),
        P(("groups", "rep"), "node", None),
        P(("groups", "rep"), "node", None),
        P(("groups", "rep"), "node"),
        P(("groups", "rep"), None),
        P(),
        P(),
        P(),
        P(),
        P(),
    )
    out_specs = (
        P(("groups", "rep"), "node", None),
        P(("groups", "rep"), "node", None),
        P("groups", None),
        P("groups", None),
        P("groups", None),
        P("groups", None),
    )
    return jax.shard_map(
        on_device, mesh=mesh, in_specs=in_specs, out_specs=out_specs, check_vma=False
    )
```

profile of v0, /device:TPU:0, one launch (start us, length us, event | category | flops | bytes accessed | tf_op | source)
XLA Modules:
  0.0 189.7 jit_solution(12456625626089858018)
XLA Ops:
  7.3 0.6 copy-done.12
  8.0 0.7 copy-done.10
  8.9 0.6 copy-done.13
  9.5 1.0 fusion.42
  11.0 0.6 copy-done.11
  11.6 0.6 convolution_bitcast_fusion
  13.4 0.3 convolution_convert_fusion.3
  13.6 0.3 copy-done.5
  14.1 0.2 convolution_convert_fusion.1
  14.4 15.6 %all_gather.7 = bf16[512,256]{1,0:T(8,128)(2,1)S(1)} all-gather(bf16[128,256]{1,0:T(8,128)(2,1)S(1)} %convolution_convert_fusion.1), channel_id=1, replica_groups=mesh['groups'=2,'node'=4,'rep'=4] {'node'}, dimensions={0}, use_global_device_ids=true | all-gather | bytes 327680 | tf_op jit(solution)/shard_map/all_gather | solution.py:89
  30.0 14.6 %all_gather.6 = bf16[512,256]{1,0:T(8,128)(2,1)S(1)} all-gather(bf16[128,256]{1,0:T(8,128)(2,1)S(1)} %convolution_convert_fusion.2), channel_id=1, replica_groups=mesh['groups'=2,'node'=4,'rep'=4] {'node'}, dimensions={0}, use_global_device_ids=true | all-gather | bytes 327680 | tf_op jit(solution)/shard_map/all_gather | solution.py:88
  44.6 0.4 fusion.46
  45.0 0.4 fusion.43
  45.4 0.3 fusion.124
  45.7 0.4 fusion.127
  46.0 0.4 fusion.44
  46.4 0.3 fusion.126
  46.7 0.4 fusion.45
  47.1 0.4 fusion.125
  47.5 0.4 select_reduce_fusion.3
  47.9 0.3 select_convert_fusion.3
  48.2 0.3 convolution_convert_fusion.10
  48.7 0.3 convolution_convert_fusion.8
  49.0 0.4 copy-done.3
  49.9 0.2 multiply_reduce_fusion.3
  50.3 0.3 fusion.14
  50.8 0.3 fusion.16
  51.3 0.3 fusion.21
  51.8 0.3 fusion.25
  52.7 1.0 copy.27
  54.0 0.3 fusion.31
  54.3 0.3 fusion.33
  54.8 0.2 fusion.105
  55.0 1.0 fusion.50
  56.0 1.1 fusion.104
  57.1 19.4 %reduce-scatter.4.cloned.1.call-done = bf16[128,512]{1,0:T(8,128)(2,1)} async-done(((bf16[512,512]{1,0:T(8,128)(2,1)}), bf16[128,512]{1,0:T(8,128)(2,1)}) %reduce-scatter.4.cloned.1.call-update) | async-done | bytes 131088
  76.5 2.0 %fusion.78 = f32[512,256]{1,0:T(8,128)} fusion(bf16[128,512]{1,0:T(8,128)(2,1)} %reduce-scatter.4.cloned.1.call-done, bf16[1,128,512]{2,1,0:T(8,128)(2,1)S(1)} %copy-done.1, f32[128]{0:T(128)S(1)} %add_rsqrt_fusion), kind=kOutput, calls=%fused_computation.125 | convolution fusion | flops 33751040 | bytes 721408 | tf_op jit(solution)/shard_map/dot_general | solution.py:18
  78.5 1.1 fusion.75
  79.6 0.9 fusion.17
  80.7 0.3 fusion.37
  81.1 0.8 fusion.49
  81.9 95.8 %all-reduce.3.cloned.1.call-done = (f32[512,256]{1,0:T(8,128)}, f32[512,256]{1,0:T(8,128)}, f32[512,256]{1,0:T(8,128)}, f32[256,512]{1,0:T(8,128)}) async-done(((f32[512,256]{1,0:T(8,128)}, f32[512,256]{1,0:T(8,128)}, f32[512,256]{1,0:T(8,128)}, f32[256,512]{1,0:T(8,128)}), (f32[512,256]{1,0:T(8,128)}, f32[512,256]{1,0:T(8,128)}, f32[512,256]{1,0:T(8,128)}, ...) | async-done | bytes 2097168 | tf_op jit(solution)/shard_map/psum | solution.py:183
  177.7 1.9 %copy.53 = f32[512,256]{1,0:T(8,128)} copy(f32[512,256]{1,0:T(8,128)} %get-tuple-element.43) | data formatting | bytes 1048576
  179.6 0.8 copy.54
  180.4 0.4 copy-done.7
  180.8 0.8 copy.55
  181.6 0.4 copy-done.6
  182.0 0.8 copy.56
  (60 shorter events, 5.0 us)
Async XLA Ops:
  7.2 7.0 %copy-start = (bf16[512,256]{1,0:T(8,128)(2,1)S(1)}, bf16[512,256]{1,0:T(8,128)(2,1)}, u32[]{:S(2)}) copy-start(bf16[512,256]{1,0:T(8,128)(2,1)} %param.17) | copy-start | bytes 786436
  7.2 69.3 %reduce-scatter.4.cloned.1.call-start = ((), (), s32[]{:S(2)}) async-start(), calls=%async_computation.1 | async-start | bytes 655360
  7.3 0.7 copy-start.12
  8.0 0.7 copy-start.10
  8.8 0.7 copy-start.13
  10.9 0.7 copy-start.11
  11.6 1.7 copy-start.4
  12.3 1.0 copy-start.1
  12.9 1.0 copy-start.5
  48.5 1.0 copy-start.3
  48.7 0.9 copy-start.2
  53.7 123.9 %all-reduce.3.cloned.1.call-start = ((), (), s32[]{:S(2)}) async-start(), calls=%async_computation.2 | async-start | bytes 4194304 | tf_op jit(solution)/shard_map/psum | solution.py:183
  76.5 2.0 %copy-start.9 = (bf16[128,512]{1,0:T(8,128)(2,1)S(1)}, bf16[128,512]{1,0:T(8,128)(2,1)}, u32[]{:S(2)}) copy-start(bf16[128,512]{1,0:T(8,128)(2,1)} %reduce-scatter.4.cloned.1.call-done) | copy-start | bytes 393220
  177.6 1.9 %copy-start.8 = (f32[512,256]{1,0:T(8,128)S(1)}, f32[512,256]{1,0:T(8,128)}, u32[]{:S(2)}) copy-start(f32[512,256]{1,0:T(8,128)} %get-tuple-element.44) | copy-start | bytes 1572868
  179.6 1.2 copy-start.7
  180.8 1.2 copy-start.6
Sparse Core Ops, SparseCore 0:
  53.8 22.5 reduce-scatter.3
  81.0 96.5 all-reduce.2
where the time goes:
time: 190 us
  waiting for transfers between devices  115 us (61%)
  blocking collectives  30.2 us (16%)
  matrix products  16.7 us (9%)
  between operations  14.3 us (8%)
  local copies, waits for them, and re-layouts  10.3 us (5%)
  other arithmetic  2.95 us (2%)
    psum x1, waiting for transfers between devices, on_device(): lax.psum((partial_query, partial_key, partial_value, partial_out), ('node...  95.8 us
    unnamed x3, waiting for transfers between devices  19.4 us
    all_gather x1, blocking collectives, on_device(): lax.all_gather(values, 'node', axis=0, tiled=True)  15.6 us
    all_gather x1, blocking collectives, on_device(): lax.all_gather(keys, 'node', axis=0, tiled=True)  14.6 us
    unnamed x33, local copies, waits for them, and re-layouts  9.64 us
    dot_general x12, matrix products, rows_product(): lax.dot_general(left, right, CONTRACT_ROWS, preferred_element_type=jnp.fl...  6.81 us
  transfers between devices with their start and end apart: 2, of which 2 were waited for; matrix products, arithmetic and copies ran while one was open for 3% of the time, Pallas kernels for 0%

commit v1 on v0

--- a/solution.py
+++ b/solution.py
@@ -12,6 +12,18 @@
 HIGH = lax.Precision.HIGHEST
 CONTRACT_ROWS = (((0,), (0,)), ((), ()))
 CONTRACT_COLS = (((1,), (1,)), ((), ()))
+
+
+def collect(x, axis, dim):
+    ways, here, step = (lax.axis_size(axis), lax.axis_index(axis), x.shape[dim])
+    line, have = (x, 1)
+    while have < ways:
+        line = jnp.concatenate(
+            [line, lax.ppermute(line, axis, [(d, (d - have) % ways) for d in range(ways)])],
+            axis=dim,
+        )
+        have = 2 * have
+    return jnp.roll(line, here * step, axis=dim)
 
 
 def rows_product(left, right):
@@ -85,7 +97,7 @@
         jnp.bfloat16
     )
     keys_all, values_all = (
-        lax.all_gather(keys, "node", axis=0, tiled=True),
+        collect(keys, "node", 0),
         lax.all_gather(values, "node", axis=0, tiled=True),
     )
     levels, onehot, level_bias = level_tables(starts, total, bias_table)

time: 190 us -> 183 us (0.963)
  blocking collectives: 30.2 us -> 16 us
  starting transfers between devices: 0.08 us -> 5.18 us
  waiting for transfers between devices: 115 us -> 112 us
  local copies, waits for them, and re-layouts: 10.3 us -> 12.5 us
    all_gather x1 -> x0, blocking collectives: 14.6 us -> none  [on_device(): lax.all_gather(keys, 'node', axis=0, tiled=True)]
    ppermute x0 -> x2, starting transfers between devices: none -> 5.1 us  [collect(): lax.ppermute(line, axis, [(d, (d - have) % ways) for d in range(ways)])]
    unnamed x3, waiting for transfers between devices: 19.4 us -> 16.3 us
    unnamed x33 -> x55, local copies, waits for them, and re-layouts: 9.64 us -> 11 us
  transfers between devices with their start and end apart: 2 -> 4, of which waited for: 2 -> 2; matrix products, arithmetic and copies ran while one was open for 3% -> 5% of each run, Pallas kernels for 0% -> 0%
where the time goes in v1:
time: 183 us; the launch traced here: 182 us
  waiting for transfers between devices  112 us (61%)
  matrix products  18.5 us (10%)
  blocking collectives  16 us (9%)
  between operations  14.5 us (8%)
  local copies, waits for them, and re-layouts  12.5 us (7%)
  starting transfers between devices  5.18 us (3%)
  other arithmetic  3.66 us (2%)
    psum x1, waiting for transfers between devices, on_device(): lax.psum((partial_query, partial_key, partial_value, partial_out), ('node...  95.7 us
    unnamed x3, waiting for transfers between devices  16.3 us
    all_gather x1, blocking collectives, on_device(): lax.all_gather(values, 'node', axis=0, tiled=True)  16 us
    unnamed x55, local copies, waits for them, and re-layouts  11 us
    dot_general x12, matrix products, rows_product(): lax.dot_general(left, right, CONTRACT_ROWS, preferred_element_type=jnp.fl...  6.82 us
    ppermute x2, starting transfers between devices, collect(): lax.ppermute(line, axis, [(d, (d - have) % ways) for d in range(ways)])  5.1 us
  transfers between devices with their start and end apart: 4, of which 2 were waited for; matrix products, arithmetic and copies ran while one was open for 5% of the time, Pallas kernels for 0%

profile of v1, /device:TPU:0, one launch (start us, length us, event | category | flops | bytes accessed | tf_op | source)
XLA Modules:
  0.0 182.3 jit_solution(12391006468084200230)
XLA Ops:
  7.2 1.1 fusion.42
  8.6 5.1 %collective-permute-start = (bf16[128,256]{1,0:T(8,128)(2,1)S(1)}, bf16[128,256]{1,0:T(8,128)(2,1)S(1)}, u32[]{:S(2)}, u32[]{:S(2)}) collective-permute-start(bf16[128,256]{1,0:T(8,128)(2,1)S(1)} %get-tuple-element.27), channel_id=1, source_target_pairs={{0,12},{4,0},{8,4},{12,8},{1,13},{5,1},{9,5},{13,9},{2,14},{6,2},{... | collective-permute-start | bytes 196616 | tf_op jit(solution)/shard_map/ppermute | solution.py:22
  13.7 0.7 copy-done.21
  14.4 0.6 copy-done.22
  15.2 0.5 copy-done.20
  15.7 0.6 convolution_bitcast_fusion
  17.9 0.4 fusion.46
  18.3 0.4 fusion.43
  18.7 0.4 fusion.44
  19.2 0.4 fusion.45
  19.6 0.7 copy-done.19
  20.6 0.7 pad_maximum_fusion
  21.3 16.0 %all_gather.3 = bf16[512,256]{1,0:T(8,128)(2,1)S(1)} all-gather(bf16[128,256]{1,0:T(8,128)(2,1)S(1)} %convolution_convert_fusion.1), channel_id=1, replica_groups=mesh['groups'=2,'node'=4,'rep'=4] {'node'}, dimensions={0}, use_global_device_ids=true | all-gather | bytes 327680 | tf_op jit(solution)/shard_map/all_gather | solution.py:101
  37.8 0.9 constant_dynamic-update-slice_fusion.3
  38.8 0.9 constant_dynamic-update-slice_fusion
  39.7 0.3 fusion.126
  40.0 0.3 fusion.128
  40.2 0.4 fusion.127
  40.6 0.4 fusion.129
  41.0 0.4 select_reduce_fusion.3
  41.4 0.3 select_convert_fusion.3
  41.7 0.3 convolution_convert_fusion.10
  42.2 0.3 convolution_convert_fusion.8
  42.5 0.3 copy-done.10
  42.8 0.8 multiply_reduce_fusion.3
  43.9 0.8 fusion.30
  45.2 0.9 fusion.31
  46.6 0.3 fusion.21
  47.1 0.3 fusion.25
  48.0 1.0 copy.27
  49.0 0.3 fusion.33
  49.6 0.5 copy-done.14
  50.3 0.5 copy-done.11
  50.8 1.0 fusion.50
  51.8 1.1 fusion.104
  52.9 16.2 %reduce-scatter.4.cloned.1.call-done = bf16[128,512]{1,0:T(8,128)(2,1)} async-done(((bf16[512,512]{1,0:T(8,128)(2,1)}), bf16[128,512]{1,0:T(8,128)(2,1)}) %reduce-scatter.4.cloned.1.call-update) | async-done | bytes 131088
  69.2 2.0 %fusion.78 = f32[512,256]{1,0:T(8,128)} fusion(bf16[128,512]{1,0:T(8,128)(2,1)} %reduce-scatter.4.cloned.1.call-done, bf16[1,128,512]{2,1,0:T(8,128)(2,1)S(1)} %copy-done.1, f32[128]{0:T(128)S(1)} %copy-done.18), kind=kOutput, calls=%fused_computation.126 | convolution fusion | flops 33751040 | bytes 721408 | tf_op jit(solution)/shard_map/dot_general | solution.py:30
  71.2 1.1 fusion.75
  72.4 0.9 fusion.17
  73.5 0.3 fusion.37
  73.8 0.8 fusion.49
  74.6 95.7 %all-reduce.3.cloned.1.call-done = (f32[512,256]{1,0:T(8,128)}, f32[512,256]{1,0:T(8,128)}, f32[512,256]{1,0:T(8,128)}, f32[256,512]{1,0:T(8,128)}) async-done(((f32[512,256]{1,0:T(8,128)}, f32[512,256]{1,0:T(8,128)}, f32[512,256]{1,0:T(8,128)}, f32[256,512]{1,0:T(8,128)}), (f32[512,256]{1,0:T(8,128)}, f32[512,256]{1,0:T(8,128)}, f32[512,256]{1,0:T(8,128)}, ...) | async-done | bytes 2097168 | tf_op jit(solution)/shard_map/psum | solution.py:195
  170.3 1.9 %copy.58 = f32[512,256]{1,0:T(8,128)} copy(f32[512,256]{1,0:T(8,128)} %get-tuple-element.45) | data formatting | bytes 1048576
  172.2 0.8 copy.59
  173.0 0.4 copy-done.7
  173.4 0.8 copy.60
  174.2 0.4 copy-done.6
  174.7 0.8 copy.61
  (87 shorter events, 6.0 us)
Async XLA Ops:
  7.2 1.1 copy-start
  7.2 1.1 copy-start.1
  7.2 62.0 %reduce-scatter.4.cloned.1.call-start = ((), (), s32[]{:S(2)}) async-start(), calls=%async_computation.1 | async-start | bytes 655360
  8.3 9.3 %copy-start.17 = (f32[128]{0:T(128)}, f32[128]{0:T(128)S(1)}, u32[]{:S(2)}) copy-start(f32[128]{0:T(128)S(1)} %add_rsqrt_fusion) | copy-start | bytes 1540
  8.3 8.0 %copy-start.5 = (bf16[512,256]{1,0:T(8,128)(2,1)S(1)}, bf16[512,256]{1,0:T(8,128)(2,1)}, u32[]{:S(2)}) copy-start(bf16[512,256]{1,0:T(8,128)(2,1)} %param.15) | copy-start | bytes 786436
  8.6 12.0 %collective-permute-start = (bf16[128,256]{1,0:T(8,128)(2,1)S(1)}, bf16[128,256]{1,0:T(8,128)(2,1)S(1)}, u32[]{:S(2)}, u32[]{:S(2)}) collective-permute-start(bf16[128,256]{1,0:T(8,128)(2,1)S(1)} %get-tuple-element.27), channel_id=1, source_target_pairs={{0,12},{4,0},{8,4},{12,8},{1,13},{5,1},{9,5},{13,9},{2,14},{6,2},{... | collective-permute-start | bytes 196616 | tf_op jit(solution)/shard_map/ppermute | solution.py:22
  13.7 0.7 copy-start.21
  14.4 0.7 copy-start.22
  15.0 0.7 copy-start.20
  16.4 1.3 copy-start.3
  18.7 1.6 copy-start.4
  19.1 1.2 copy-start.2
  19.6 0.7 copy-start.19
  21.3 16.5 %collective-permute-start.1 = (bf16[256,256]{1,0:T(8,128)(2,1)}, bf16[256,256]{1,0:T(8,128)(2,1)}, u32[]{:S(2)}, u32[]{:S(2)}) collective-permute-start(bf16[256,256]{1,0:T(8,128)(2,1)} %pad_maximum_fusion), channel_id=1, source_target_pairs={{0,8},{4,12},{8,0},{12,4},{1,9},{5,13},{9,1},{13,5},{2,10},{6,14},... | collective-permute-start | bytes 393224 | tf_op jit(solution)/shard_map/ppermute | solution.py:22
  42.2 0.6 copy-start.10
  42.5 1.2 copy-start.12
  49.0 121.3 %all-reduce.3.cloned.1.call-start = ((), (), s32[]{:S(2)}) async-start(), calls=%async_computation.2 | async-start | bytes 4194304 | tf_op jit(solution)/shard_map/psum | solution.py:195
  49.3 0.7 copy-start.14
  49.3 0.7 copy-start.15
  50.1 0.7 copy-start.11
  50.1 0.7 copy-start.13
  50.1 0.7 copy-start.16
  50.8 1.0 copy-start.18
  69.2 2.0 %copy-start.9 = (bf16[128,512]{1,0:T(8,128)(2,1)S(1)}, bf16[128,512]{1,0:T(8,128)(2,1)}, u32[]{:S(2)}) copy-start(bf16[128,512]{1,0:T(8,128)(2,1)} %reduce-scatter.4.cloned.1.call-done) | copy-start | bytes 393220
  170.3 1.9 %copy-start.8 = (f32[512,256]{1,0:T(8,128)S(1)}, f32[512,256]{1,0:T(8,128)}, u32[]{:S(2)}) copy-start(f32[512,256]{1,0:T(8,128)} %get-tuple-element.46) | copy-start | bytes 1572868
  172.2 1.2 copy-start.7
  173.4 1.2 copy-start.6
Sparse Core Ops, SparseCore 0:
  49.1 20.0 reduce-scatter.3
  73.7 96.4 all-reduce.2
